TPU v7x, 512 devices: a whole 4x4x16 slice. The times are simulated.
512 devices in a mesh: ctx: 16 (over z_lo, core), head: 32 (over z_hi, y, x).
Axes of the slice: x: 4, y: 4, z: 16 (z_hi: 2, z_lo: 8; z = z_hi * 8 + z_lo), core: 2. Of those that a mesh axis runs over, the one named last changes fastest.
Arguments:
- tokens: bfloat16 [4096, 4096], P('ctx', 'head'), may hold values from -6 to 6
- qkv_weight: bfloat16 [4096, 3, 4096], P(None, None, 'head'), may hold values from -0.09375 to 0.09375
- out_weight: bfloat16 [4096, 4096], P('head'), may hold values from -1 to 1
- signs: int32 [32, 2, 128], P('head'), may hold values from 0 to 1
- rows: int32 [32, 2, 64], P('head'), may hold values from 0 to 127
Outputs:
- mixed: bfloat16 [4096, 4096], P('ctx', 'head')
Inputs may be any that keep to these rules, and one draw needn't show every extreme that they name: `signs`: each sign bit s gives the sign 2 s - 1. `rows`: rows are drawn with repetition.
All inputs are finite; a program needn't handle non-finite values.
Results may differ from a plain program's by a relative error of at most 0.025.
Values may be sent and summed in bfloat16 or wider, within the bound.
A program may use at most 128 MiB of HBM per device.

v0:
```python
import math
import jax
import jax.numpy as jnp
from jax import lax
from jax.sharding import PartitionSpec as P

BLOCK = 256
score_scale = 2.0


def prefix(value, axis, join, neutral):
    place = lax.axis_index(axis)
    gathered = jax.tree.map(
        lambda a, kind: lax.all_gather(a.astype(kind), axis), value, (jnp.bfloat16, jnp.bfloat16)
    )
    state = jax.tree.map(lambda a, e: jnp.zeros_like(a) + jnp.asarray(e, a.dtype), value, neutral)

    def one(hop, state):
        return join(
            state,
            jax.tree.map(
                lambda a, own: lax.dynamic_index_in_dim(a, hop, 0, False).astype(own.dtype),
                gathered,
                value,
            ),
        )

    return lax.fori_loop(0, place, one, state)


def hadamard_table(size_hd):
    row_index = jnp.arange(size_hd, dtype=jnp.int32)[:, None]
    col_index = jnp.arange(size_hd, dtype=jnp.int32)[None, :]
    common = jnp.bitwise_and(row_index, col_index)
    parity = jnp.zeros((size_hd, size_hd), jnp.int32)
    for bit_place in range(size_hd.bit_length() - 1):
        parity = parity + jnp.bitwise_and(jnp.right_shift(common, bit_place), 1)
    return 1.0 - 2.0 * jnp.bitwise_and(parity, 1).astype(jnp.float32)


def sketch_matrix(signs, rows):
    size_hd = signs.shape[-1]
    hadamard = hadamard_table(size_hd)
    selector = (jnp.arange(size_hd, dtype=jnp.int32)[:, None] == rows[..., None, :]).astype(
        jnp.float32
    )
    columns = jnp.einsum("de,kief->kidf", hadamard, selector, precision=lax.Precision.HIGHEST)
    signed = (2 * signs - 1).astype(jnp.float32)
    return (signed[..., None] * columns).astype(jnp.bfloat16)


def normalize(raw_rows):
    scale_rows = lax.rsqrt(jnp.mean(raw_rows * raw_rows, axis=-1, keepdims=True) + 1e-06)
    return (raw_rows * scale_rows).astype(jnp.bfloat16)


def features(normed, sketch):
    size_hd = sketch.shape[2]
    size_m = sketch.shape[3]
    branches = jnp.einsum("tkd,kidm->tkim", normed, sketch, preferred_element_type=jnp.float32)
    factor = score_scale * score_scale / (size_hd * math.sqrt(size_m))
    sketched = factor * branches[:, :, 0, :] * branches[:, :, 1, :]
    squared = sketched[:, :, :, None] * sketched[:, :, None, :]
    return squared.reshape(sketched.shape[0], sketched.shape[1], size_m * size_m).astype(
        jnp.bfloat16
    )


def add_pair(earlier, later):
    return (earlier[0] + later[0], earlier[1] + later[1])


def shards(tokens, qkv_weight, out_weight, signs, rows):
    length = tokens.shape[0]
    local_heads = signs.shape[0]
    size_hd = signs.shape[2]
    model_width = qkv_weight.shape[0]
    flat_weight = qkv_weight.reshape(model_width, 3 * local_heads * size_hd)
    projected = jnp.dot(
        lax.all_gather(tokens, "head", axis=1, tiled=True),
        flat_weight,
        preferred_element_type=jnp.float32,
    )
    projected = projected.reshape(length, 3, local_heads, size_hd)
    normed_queries = normalize(projected[:, 0])
    normed_keys = normalize(projected[:, 1])
    values = projected[:, 2].astype(jnp.bfloat16)
    sketch = sketch_matrix(signs, rows)
    query_feats = features(normed_queries, sketch)
    key_feats = features(normed_keys, sketch)
    feat_width = query_feats.shape[2]
    nblocks = length // BLOCK
    qf = query_feats.reshape(nblocks, BLOCK, local_heads, feat_width)
    kf = key_feats.reshape(nblocks, BLOCK, local_heads, feat_width)
    vbk = values.reshape(nblocks, BLOCK, local_heads, size_hd)
    block_states = jnp.einsum("btkf,btkd->bkfd", kf, vbk, preferred_element_type=jnp.float32)
    block_sums = jnp.sum(kf, axis=1, dtype=jnp.float32)
    state_zero = jnp.zeros((local_heads, feat_width, size_hd), jnp.float32)
    sum_zero = jnp.zeros((local_heads, feat_width), jnp.float32)
    local_state = jnp.sum(block_states, axis=0)
    local_sum = jnp.sum(block_sums, axis=0)
    earlier_state, earlier_sum = prefix(
        (local_state, local_sum), "ctx", add_pair, (state_zero, sum_zero)
    )
    inner_state = jnp.concatenate([state_zero[None], jnp.cumsum(block_states, axis=0)[:-1]], axis=0)
    inner_sum = jnp.concatenate([sum_zero[None], jnp.cumsum(block_sums, axis=0)[:-1]], axis=0)
    prefix_state = (earlier_state[None] + inner_state).astype(jnp.bfloat16)
    prefix_sum = (earlier_sum[None] + inner_sum).astype(jnp.bfloat16)
    num_state = jnp.einsum("btkf,bkfd->btkd", qf, prefix_state, preferred_element_type=jnp.float32)
    den_state = jnp.einsum("btkf,bkf->btk", qf, prefix_sum, preferred_element_type=jnp.float32)
    qblk = normed_queries.reshape(nblocks, BLOCK, local_heads, size_hd)
    kblk = normed_keys.reshape(nblocks, BLOCK, local_heads, size_hd)
    scores = jnp.einsum("btkd,bpkd->bktp", qblk, kblk, preferred_element_type=jnp.float32)
    causal = (
        jnp.arange(BLOCK, dtype=jnp.int32)[:, None] >= jnp.arange(BLOCK, dtype=jnp.int32)[None, :]
    ).astype(jnp.float32)
    weights = (score_scale * scores / size_hd) ** 4 * causal[None, None]
    den_diag = jnp.sum(weights, axis=-1).transpose(0, 2, 1)
    weights_b = weights.astype(jnp.bfloat16)
    num_diag = jnp.einsum("bktp,bpkd->btkd", weights_b, vbk, preferred_element_type=jnp.float32)
    attended = (num_diag + num_state) / (1.0 + den_diag + den_state)[..., None]
    attended = attended.astype(jnp.bfloat16).reshape(length, local_heads * size_hd)
    partial_out = jnp.dot(attended, out_weight, preferred_element_type=jnp.float32)
    mixed = lax.psum_scatter(
        partial_out.astype(jnp.bfloat16), "head", scatter_dimension=1, tiled=True
    )
    return mixed


def solution(mesh):
    in_specs = (
        P("ctx", "head"),
        P(None, None, "head"),
        P("head", None),
        P("head", None, None),
        P("head", None, None),
    )
    out_specs = P("ctx", "head")
    return jax.shard_map(shards, mesh=mesh, in_specs=in_specs, out_specs=out_specs, check_vma=False)
```

profile of v0, /device:TPU:96, one launch (start us, length us, event | category | flops | bytes accessed | tf_op | source)
XLA Modules:
  0.0 710.8 jit_solution(11091749225744624335)
XLA Ops:
  6.5 0.7 all-gather.4.cloned.1.call-update
  7.3 4.7 copy.17
  12.0 0.3 fusion.14
  12.3 146.7 %all-gather.4.cloned.1.call-done = bf16[256,4096]{1,0:T(8,128)(2,1)} async-done(((bf16[256,128]{1,0:T(8,128)(2,1)}), bf16[256,4096]{1,0:T(8,128)(2,1)}) %all-gather.4.cloned.1.call-update) | async-done | bytes 2097168 | tf_op jit(solution)/shard_map/all_gather | solution.py:80
  159.0 3.5 fusion.3
  162.6 0.1 convolution_bitcast_fusion.1
  162.8 0.7 multiply_convert_fusion.1
  163.4 1.7 convolution_convert_fusion.1
  165.2 0.6 fusion.21
  165.9 23.1 %all_gather.13 = bf16[16,1,4096]{2,1,0:T(2,128)(2,1)} all-gather(bf16[1,1,4096]{2,1,0:T(2,128)(2,1)S(1)} %convert_element_type.187), channel_id=1, replica_groups=mesh['ctx'=16,'head'=32] {'ctx'}, dimensions={0}, use_global_device_ids=true | all-gather | bytes 139264 | tf_op jit(solution)/shard_map/all_gather | solution.py:14
  189.2 1.5 fusion.85
  190.6 2.0 multiply_convert_fusion
  192.7 153.7 %all-gather.6.cloned.1.call-done = bf16[65536,128]{1,0:T(8,128)(2,1)} async-done(((bf16[4096,128]{1,0:T(8,128)(2,1)}), bf16[65536,128]{1,0:T(8,128)(2,1)}) %all-gather.6.cloned.1.call-update) | async-done | bytes 16777232 | tf_op jit(solution)/shard_map/all_gather | solution.py:14
  346.5 13.7 %while.12 = (s32[]{:T(128)}, f32[1,4096,128]{2,1,0:T(8,128)S(1)}, f32[1,4096]{1,0:T(1,128)S(1)}, s32[]{:T(128)}, bf16[16,1,4096,128]{3,2,1,0:T(8,128)(2,1)}, /*i...) while((s32[]{:T(128)}, f32[1,4096,128]{2,1,0:T(8,128)S(1)}, f32[1,4096]{1,0:T(1,128)S(1)}, ...), condition=%wide.region_4.0_spmd, body=%wide.region_3.0_spmd.sunk | while | flops 1056773 | bytes 5283975 | solution.py:28
  346.6 1.5 convert_add_fusion.4
  348.1 0.8 convert_add_fusion.5
  348.8 1.5 convert_add_fusion.4
  350.4 0.8 convert_add_fusion.5
  351.1 1.5 convert_add_fusion.4
  352.6 0.8 convert_add_fusion.5
  353.4 1.5 convert_add_fusion.4
  354.9 0.8 convert_add_fusion.5
  355.7 1.5 convert_add_fusion.4
  357.2 0.8 convert_add_fusion.5
  358.0 1.5 convert_add_fusion.4
  359.5 0.8 convert_add_fusion.5
  360.3 2.1 fusion.73
  362.5 1.1 fusion.18
  363.6 1.9 convolution_convert_fusion
  365.5 2.5 copy.25
  368.0 334.7 %reduce-scatter.4.cloned.1.call-done = bf16[128,256]{1,0:T(8,128)(2,1)} async-done(((bf16[4096,256]{1,0:T(8,128)(2,1)}), bf16[128,256]{1,0:T(8,128)(2,1)}) %reduce-scatter.4.cloned.1.call-update) | async-done | bytes 65552
  702.7 1.6 copy.26
  (25 shorter events, 0.7 us)
Async XLA Ops:
  6.5 357.1 %copy-start = (bf16[128,4096]{1,0:T(8,128)(2,1)S(1)}, bf16[128,4096]{1,0:T(8,128)(2,1)}, u32[]{:S(2)}) copy-start(bf16[128,4096]{1,0:T(8,128)(2,1)} %param.9) | copy-start | bytes 3145732
  6.5 152.5 %all-gather.4.cloned.1.call-start = ((), (), s32[]{:S(2)}) async-start(), calls=%async_computation.1 | async-start | bytes 2162688 | tf_op jit(solution)/shard_map/all_gather | solution.py:80
  7.3 4.8 copy-start.3
  7.3 4.8 copy-start.4
  7.3 339.1 %all-gather.6.cloned.1.call-start = ((), (), s32[]{:S(2)}) async-start(), calls=%async_computation.2 | async-start | bytes 17825792 | tf_op jit(solution)/shard_map/all_gather | solution.py:14
  165.2 537.5 %reduce-scatter.4.cloned.1.call-start = ((), (), s32[]{:S(2)}) async-start(), calls=%async_computation.3 | async-start | bytes 2162688
  360.3 2.2 copy-start.1
  362.5 1.2 copy-start.2
Sparse Core Ops, SparseCore 0:
  11.4 147.5 all-gather.3
  165.3 181.0 all-gather.5
  368.1 334.5 reduce-scatter.3
where the time goes:
time: 712 us; the launch traced here: 711 us
  waiting for transfers between devices  636 us (89%)
  blocking collectives  23.1 us (3%)
  other arithmetic  17 us (2%)
  between operations  13.2 us (2%)
  matrix products  12.4 us (2%)
  local copies, waits for them, and re-layouts  9.08 us (1%)
    unnamed x4, waiting for transfers between devices  335 us
    all_gather x1, waiting for transfers between devices, prefix(): lax.all_gather(a.astype(kind), axis)  154 us
    all_gather x1, waiting for transfers between devices, shards(): lax.all_gather(tokens, 'head', axis=1, tiled=True)  147 us
    all_gather x1, blocking collectives, prefix(): lax.all_gather(a.astype(kind), axis)  23.1 us
  transfers between devices with their start and end apart: 3, of which 3 were waited for; matrix products, arithmetic and copies ran while one was open for 1% of the time, Pallas kernels for 0%

commit v1 on v0

--- a/solution.py
+++ b/solution.py
@@ -76,11 +76,15 @@
     size_hd = signs.shape[2]
     model_width = qkv_weight.shape[0]
     flat_weight = qkv_weight.reshape(model_width, 3 * local_heads * size_hd)
-    projected = jnp.dot(
-        lax.all_gather(tokens, "head", axis=1, tiled=True),
-        flat_weight,
-        preferred_element_type=jnp.float32,
-    )
+
+    def track_shelves(local_block, link_axis="head"):
+        e_now = lax.axis_size(link_axis)
+        everything = jnp.stack(e_now * [local_block])
+        local_now = lax.all_to_all(everything, split_axis=0, concat_axis=0, axis_name=link_axis)
+        a_next = jnp.concatenate(local_now, axis=1)
+        return a_next
+
+    projected = jnp.dot(track_shelves(tokens), flat_weight, preferred_element_type=jnp.float32)
     projected = projected.reshape(length, 3, local_heads, size_hd)
     normed_queries = normalize(projected[:, 0])
     normed_keys = normalize(projected[:, 1])

time: 712 us -> 687 us (0.965)
  waiting for transfers between devices: 636 us -> 585 us
  starting transfers between devices: 0.08 us -> 18 us
  local copies, waits for them, and re-layouts: 9.08 us -> 17.4 us
    all_gather x1 -> x0, waiting for transfers between devices: 147 us -> none  [shards(): lax.all_gather(tokens, 'head', axis=1, tiled=True)]
    all_to_all x0 -> x1, waiting for transfers between devices: none -> 94.6 us  [track_shelves(): lax.all_to_all(everything, split_axis=0, concat_axis=0, axis_name=link_axis)]
    all_to_all x0 -> x1, starting transfers between devices: none -> 17.9 us  [track_shelves(): lax.all_to_all(everything, split_axis=0, concat_axis=0, axis_name=link_axis)]
    unnamed x4 -> x3, waiting for transfers between devices: 335 us -> 333 us
where the time goes in v1:
time: 687 us; the launch traced here: 685 us
  waiting for transfers between devices  585 us (85%)
  blocking collectives  21.3 us (3%)
  starting transfers between devices  18 us (3%)
  local copies, waits for them, and re-layouts  17.4 us (3%)
  other arithmetic  17 us (2%)
  between operations  13.6 us (2%)
  matrix products  12.4 us (2%)
    unnamed x3, waiting for transfers between devices  333 us
    all_gather x1, waiting for transfers between devices, prefix(): lax.all_gather(a.astype(kind), axis)  158 us
    all_to_all x1, waiting for transfers between devices, track_shelves(): lax.all_to_all(everything, split_axis=0, concat_axis=0, axis_name=link_axis)  94.6 us
    all_gather x1, blocking collectives, prefix(): lax.all_gather(a.astype(kind), axis)  21.3 us
    all_to_all x1, starting transfers between devices, track_shelves(): lax.all_to_all(everything, split_axis=0, concat_axis=0, axis_name=link_axis)  17.9 us
  transfers between devices with their start and end apart: 3, of which 3 were waited for; matrix products, arithmetic and copies ran while one was open for 1% of the time, Pallas kernels for 0%

profile of v1, /device:TPU:96, one launch (start us, length us, event | category | flops | bytes accessed | tf_op | source)
XLA Modules:
  0.0 685.0 jit_solution(2869411239764129456)
XLA Ops:
  6.5 2.7 stack.2
  9.3 17.9 %all-to-all-start = ((bf16[32,256,128]{2,1,0:T(8,128)(2,1)}), bf16[32,256,128]{2,1,0:T(8,128)(2,1)S(1)}, u32[]{:S(2)}, u32[]{:S(2)}) async-start(bf16[32,256,128]{2,1,0:T(8,128)(2,1)} %stack.2), calls=%async_computation | async-start | bytes 4194304 | tf_op jit(solution)/shard_map/all_to_all | solution.py:83
  27.2 4.7 copy.18
  32.0 0.9 fusion.11
  32.8 94.6 %all-to-all-done = bf16[32,256,128]{2,1,0:T(8,128)(2,1)S(1)} async-done(((bf16[32,256,128]{2,1,0:T(8,128)(2,1)}), bf16[32,256,128]{2,1,0:T(8,128)(2,1)S(1)}, u32[]{:S(2)}, u32[]{:S(2)}) %all-to-all-start) | async-done | bytes 2097184 | tf_op jit(solution)/shard_map/all_to_all | solution.py:83
  127.5 2.7 copy.17
  130.2 2.8 reshape.342
  133.0 2.9 fusion.2
  136.9 1.7 convolution_convert_fusion.1
  139.4 21.3 %all_gather.9 = bf16[16,1,4096]{2,1,0:T(2,128)(2,1)} all-gather(bf16[1,1,4096]{2,1,0:T(2,128)(2,1)S(1)} %convert_element_type.187), channel_id=1, replica_groups=mesh['ctx'=16,'head'=32] {'ctx'}, dimensions={0}, use_global_device_ids=true | all-gather | bytes 139264 | tf_op jit(solution)/shard_map/all_gather | solution.py:14
  160.8 1.5 fusion.82
  162.3 2.0 multiply_convert_fusion
  164.3 157.7 %all-gather.3.cloned.1.call-done = bf16[65536,128]{1,0:T(8,128)(2,1)} async-done(((bf16[4096,128]{1,0:T(8,128)(2,1)}), bf16[65536,128]{1,0:T(8,128)(2,1)}) %all-gather.3.cloned.1.call-update) | async-done | bytes 16777232 | tf_op jit(solution)/shard_map/all_gather | solution.py:14
  322.2 13.7 %while.12 = (s32[]{:T(128)}, f32[1,4096,128]{2,1,0:T(8,128)S(1)}, f32[1,4096]{1,0:T(1,128)S(1)}, s32[]{:T(128)}, bf16[16,1,4096,128]{3,2,1,0:T(8,128)(2,1)}, /*i...) while((s32[]{:T(128)}, f32[1,4096,128]{2,1,0:T(8,128)S(1)}, f32[1,4096]{1,0:T(1,128)S(1)}, ...), condition=%wide.region_4.0_spmd, body=%wide.region_3.0_spmd.sunk | while | flops 1056773 | bytes 5283975 | solution.py:28
  322.2 1.5 convert_add_fusion.4
  323.7 0.8 convert_add_fusion.5
  324.5 1.5 convert_add_fusion.4
  326.0 0.8 convert_add_fusion.5
  326.8 1.5 convert_add_fusion.4
  328.3 0.8 convert_add_fusion.5
  329.1 1.5 convert_add_fusion.4
  330.6 0.8 convert_add_fusion.5
  331.4 1.5 convert_add_fusion.4
  332.9 0.8 convert_add_fusion.5
  333.7 1.5 convert_add_fusion.4
  335.2 0.8 convert_add_fusion.5
  335.9 2.1 fusion.70
  338.2 1.2 fusion.15
  339.3 1.9 convolution_convert_fusion
  341.2 2.5 copy.26
  343.7 332.9 %reduce-scatter.4.cloned.1.call-done = bf16[128,256]{1,0:T(8,128)(2,1)} async-done(((bf16[4096,256]{1,0:T(8,128)(2,1)}), bf16[128,256]{1,0:T(8,128)(2,1)}) %reduce-scatter.4.cloned.1.call-update) | async-done | bytes 65552
  676.6 1.6 copy.27
  (31 shorter events, 2.1 us)
Async XLA Ops:
  6.5 332.8 %copy-start = (bf16[128,4096]{1,0:T(8,128)(2,1)S(1)}, bf16[128,4096]{1,0:T(8,128)(2,1)}, u32[]{:S(2)}) copy-start(bf16[128,4096]{1,0:T(8,128)(2,1)} %param.9) | copy-start | bytes 3145732
  9.3 118.2 %all-to-all-start = ((bf16[32,256,128]{2,1,0:T(8,128)(2,1)}), bf16[32,256,128]{2,1,0:T(8,128)(2,1)S(1)}, u32[]{:S(2)}, u32[]{:S(2)}) async-start(bf16[32,256,128]{2,1,0:T(8,128)(2,1)} %stack.2), calls=%async_computation | async-start | bytes 4194304 | tf_op jit(solution)/shard_map/all_to_all | solution.py:83
  27.2 4.8 copy-start.5
  27.2 4.8 copy-start.6
  27.2 294.9 %all-gather.3.cloned.1.call-start = ((), (), s32[]{:S(2)}) async-start(), calls=%async_computation.2 | async-start | bytes 17825792 | tf_op jit(solution)/shard_map/all_gather | solution.py:14
  133.0 3.0 copy-start.2
  136.8 23.8 %copy-start.3 = (bf16[2,128,64]{1,2,0:T(8,128)(2,1)S(1)}, bf16[2,128,64]{1,2,0:T(8,128)(2,1)}, u32[]{:S(2)}) copy-start(bf16[2,128,64]{1,2,0:T(8,128)(2,1)} %fusion.11) | copy-start | bytes 98308
  138.6 538.0 %reduce-scatter.4.cloned.1.call-start = ((), (), s32[]{:S(2)}) async-start(), calls=%async_computation.3 | async-start | bytes 2162688
  335.9 2.2 copy-start.1
  338.1 1.2 copy-start.4
Sparse Core Ops, SparseCore 0:
  138.7 183.2 all-gather.2
  343.8 332.7 reduce-scatter.3
